TPU v7x, 32 devices: a whole 2x2x4 slice. The times are simulated.
32 devices in a mesh: patch: 8 (over y, x, core), group: 4 (over z).
Axes of the slice: x: 2, y: 2, z: 4, core: 2. Of those that a mesh axis runs over, the one named last changes fastest.
Arguments:
- grid_latent: bfloat16 [16384, 512], P(('patch', 'group')), may hold values from -6 to 6
- mesh_latent: bfloat16 [8192, 512], P(('patch', 'group')), may hold values from -6 to 6
- cotangent: bfloat16 [8192, 512], P(('patch', 'group')), may hold values from -6 to 6
- halo_rows: int32 [8192], P(('patch', 'group')), may hold values from 0 to 511
- encoder_sender: int32 [24576], P(('patch', 'group')), may hold values from 0 to 767
- encoder_target: int32 [24576], P(('patch', 'group')), may hold values from 0 to 255
- encoder_count: int32 [32], P(('patch', 'group')), may hold values from 96 to 768, as said below
- process_sender: int32 [24576], P(('patch', 'group')), may hold values from 0 to 319
- process_target: int32 [24576], P(('patch', 'group')), may hold values from 0 to 255
- process_count: int32 [32], P(('patch', 'group')), may hold values from 96 to 768, as said below
- encoder_source: bfloat16 [512, 512], replicated, may hold values from -0.25 to 0.25
- encoder_dest: bfloat16 [512, 512], replicated, may hold values from -0.25 to 0.25
- encoder_output: bfloat16 [512, 512], replicated, may hold values from -0.25 to 0.25
- encoder_gain: float32 [512], replicated, may hold values from 0.5 to 1.5
- process_source: bfloat16 [512, 512], replicated, may hold values from -0.25 to 0.25
- process_dest: bfloat16 [512, 512], replicated, may hold values from -0.25 to 0.25
- process_output: bfloat16 [512, 512], replicated, may hold values from -0.25 to 0.25
- process_gain: float32 [512], replicated, may hold values from 0.5 to 1.5
Outputs:
- grid_grad: bfloat16 [16384, 512], P(('patch', 'group'))
- mesh_grad: bfloat16 [8192, 512], P(('patch', 'group'))
Inputs may be any that keep to these rules, and one draw needn't show every extreme that they name: `halo_rows`: a block's entries are rows of its own grid nodes. `encoder_sender`: rows of the block's extended grid table. `encoder_target`: rows of the block's own mesh nodes. The first encoder_count slots of a block are edges, the rest padding; some block is full in every draw. `process_sender`: rows of the block's sender table: its own mesh nodes, then the coarse nodes of its group. `process_target`: rows of the block's own mesh nodes. The first process_count slots of a block are edges, the rest padding; some block is full in every draw.
All inputs are finite; a program needn't handle non-finite values.
Results may differ from a plain program's by a relative error of at most 0.01.
Values may be sent and summed in bfloat16 or wider, within the bound.
No kernel may reach another device: no remote copies, remote signals or barrier semaphores. Data moves between devices by JAX's collectives and lax.ppermute only.
A program may use at most 64 MiB of HBM per device.

v0:
```python
import jax
import jax.numpy as jnp
from jax import lax
from jax.sharding import PartitionSpec as P

EPSILON = 1e-05


def padded_2(x, sides, width):
    for axis, dim in sides:
        size, length = (lax.axis_size(axis), x.shape[dim])
        up = [(i, (i + 1) % size) for i in range(size)]
        down = [(j, i) for i, j in up]
        last = lax.slice_in_dim(x, length - width, length, axis=dim)
        initial = lax.slice_in_dim(x, 0, width, axis=dim)
        before = lax.ppermute(last, axis, up)
        after = lax.ppermute(initial, axis, down)
        x = jnp.concatenate([before, x, after], axis=dim)
    return x


def silu_slope(values):
    logistic = jax.nn.sigmoid(values)
    return logistic * (1.0 + values * (1.0 - logistic))


def norm_forward(values, norm_gain):
    center = values - jnp.mean(values, axis=-1, keepdims=True)
    inverse = lax.rsqrt(jnp.mean(center * center, axis=-1, keepdims=True) + EPSILON)
    normed = center * inverse
    return (normed * norm_gain, normed, inverse)


def norm_backward(grad_out, normed, inverse, norm_gain):
    scaled = grad_out * norm_gain
    return inverse * (
        scaled
        - jnp.mean(scaled, axis=-1, keepdims=True)
        - normed * jnp.mean(scaled * normed, axis=-1, keepdims=True)
    )


def edge_forward(source, dest_proj, sender, target, live_count, out_weight, mesh_count):
    preact = source[sender] + dest_proj[target]
    hidden = jax.nn.silu(preact).astype(jnp.bfloat16)
    message = jnp.dot(hidden, out_weight, preferred_element_type=jnp.float32).astype(jnp.bfloat16)
    live_slots = jnp.arange(sender.shape[0], dtype=jnp.int32) < live_count
    onehot = (
        (target[None, :] == jnp.arange(mesh_count, dtype=jnp.int32)[:, None]) & live_slots[None, :]
    ).astype(jnp.bfloat16)
    gathered = jnp.dot(onehot, message, preferred_element_type=jnp.float32)
    return (gathered, preact, onehot, live_slots)


def edge_backward(
    grad_gathered, preact, onehot, live_slots, sender, target, out_weight, table_rows
):
    grad_message = jnp.where(live_slots[:, None], grad_gathered[target], 0.0).astype(jnp.bfloat16)
    grad_hidden = jnp.dot(grad_message, out_weight.T, preferred_element_type=jnp.float32)
    grad_preact = (grad_hidden * silu_slope(preact)).astype(jnp.bfloat16)
    chooser = (sender[None, :] == jnp.arange(table_rows, dtype=jnp.int32)[:, None]).astype(
        jnp.bfloat16
    )
    grad_source = jnp.dot(chooser, grad_preact, preferred_element_type=jnp.float32)
    grad_dest = jnp.dot(onehot, grad_preact, preferred_element_type=jnp.float32)
    return (grad_source, grad_dest)


def encoder_pass(
    extended,
    mesh_rows,
    sender,
    target,
    live_count,
    source_weight,
    dest_weight,
    out_weight,
    norm_gain,
):
    source = jnp.dot(extended, source_weight, preferred_element_type=jnp.float32)
    dest_proj = jnp.dot(mesh_rows, dest_weight, preferred_element_type=jnp.float32)
    gathered, preact, onehot, live_slots = edge_forward(
        source, dest_proj, sender, target, live_count, out_weight, mesh_rows.shape[0]
    )
    shifted, normed, inverse = norm_forward(gathered, norm_gain)
    updated = (mesh_rows.astype(jnp.float32) + shifted).astype(jnp.bfloat16)
    return (updated, (preact, onehot, live_slots, normed, inverse))


def encoder_backward(
    grad_updated, stored, table_rows, sender, target, dest_weight, out_weight, norm_gain
):
    preact, onehot, live_slots, normed, inverse = stored
    grad_gathered = norm_backward(grad_updated, normed, inverse, norm_gain)
    grad_source, grad_dest = edge_backward(
        grad_gathered, preact, onehot, live_slots, sender, target, out_weight, table_rows
    )
    mesh_grad = grad_updated + jnp.dot(
        grad_dest.astype(jnp.bfloat16), dest_weight.T, preferred_element_type=jnp.float32
    )
    return (mesh_grad, grad_source.astype(jnp.bfloat16))


def process_grads(
    updated,
    coarse_proj,
    sender,
    target,
    live_count,
    cotangent,
    source_weight,
    dest_weight,
    out_weight,
    norm_gain,
):
    local_proj = jnp.dot(updated, source_weight, preferred_element_type=jnp.float32)
    source = jnp.concatenate([local_proj, coarse_proj], axis=0)
    dest_proj = jnp.dot(updated, dest_weight, preferred_element_type=jnp.float32)
    gathered, preact, onehot, live_slots = edge_forward(
        source, dest_proj, sender, target, live_count, out_weight, updated.shape[0]
    )
    unused, normed, inverse = norm_forward(gathered, norm_gain)
    grad_out = cotangent.astype(jnp.float32)
    grad_gathered = norm_backward(grad_out, normed, inverse, norm_gain)
    grad_source, grad_dest = edge_backward(
        grad_gathered, preact, onehot, live_slots, sender, target, out_weight, source.shape[0]
    )
    mesh_count = updated.shape[0]
    grad_local = grad_out + jnp.dot(
        grad_source[:mesh_count].astype(jnp.bfloat16),
        source_weight.T,
        preferred_element_type=jnp.float32,
    )
    grad_local = grad_local + jnp.dot(
        grad_dest.astype(jnp.bfloat16), dest_weight.T, preferred_element_type=jnp.float32
    )
    return (grad_local, grad_source[mesh_count:])


def on_device(
    grid_latent,
    mesh_latent,
    cotangent,
    halo_rows,
    encoder_sender,
    encoder_target,
    encoder_count,
    process_sender,
    process_target,
    process_count,
    encoder_source,
    encoder_dest,
    encoder_output,
    encoder_gain,
    process_source,
    process_dest,
    process_output,
    process_gain,
):
    rim_size = halo_rows.shape[0] // 2
    grid_rows = grid_latent.shape[0]
    outgoing = grid_latent[halo_rows]
    padded = padded_2(outgoing, (("patch", 0),), rim_size)
    extended = jnp.concatenate([grid_latent, padded[:rim_size], padded[3 * rim_size :]], axis=0)
    updated, stored = encoder_pass(
        extended,
        mesh_latent,
        encoder_sender,
        encoder_target,
        encoder_count[0],
        encoder_source,
        encoder_dest,
        encoder_output,
        encoder_gain,
    )
    coarse_rows = mesh_latent.shape[0] // 16
    coarse_proj = jnp.dot(
        lax.all_gather(updated[:coarse_rows], "group", axis=0, tiled=True),
        process_source,
        preferred_element_type=jnp.float32,
    )
    grad_local, grad_coarse = process_grads(
        updated,
        coarse_proj,
        process_sender,
        process_target,
        process_count[0],
        cotangent,
        process_source,
        process_dest,
        process_output,
        process_gain,
    )
    back_weight = process_source.astype(jnp.float32).T
    coarse_grad = lax.psum_scatter(
        jnp.dot(
            grad_coarse,
            back_weight,
            precision=lax.Precision.HIGHEST,
            preferred_element_type=jnp.float32,
        ),
        "group",
        scatter_dimension=0,
        tiled=True,
    )
    grad_updated = grad_local.at[:coarse_rows].add(coarse_grad)
    mesh_grad, source_grads = encoder_backward(
        grad_updated,
        stored,
        extended.shape[0],
        encoder_sender,
        encoder_target,
        encoder_dest,
        encoder_output,
        encoder_gain,
    )
    own_grad = jnp.dot(
        source_grads[:grid_rows], encoder_source.T, preferred_element_type=jnp.float32
    )
    returned = padded_2(source_grads[grid_rows:], (("patch", 0),), rim_size)
    peer_sources = jnp.concatenate([returned[:rim_size], returned[3 * rim_size :]], axis=0)
    from_peers = jnp.dot(peer_sources, encoder_source.T, preferred_element_type=jnp.float32)
    grid_grad = own_grad.at[halo_rows].add(from_peers)
    return (grid_grad.astype(jnp.bfloat16), mesh_grad.astype(jnp.bfloat16))


def solution(mesh):
    return jax.shard_map(
        on_device,
        mesh=mesh,
        in_specs=(
            P(("patch", "group"), None),
            P(("patch", "group"), None),
            P(("patch", "group"), None),
            P(("patch", "group")),
            P(("patch", "group")),
            P(("patch", "group")),
            P(("patch", "group")),
            P(("patch", "group")),
            P(("patch", "group")),
            P(("patch", "group")),
            P(),
            P(),
            P(),
            P(),
            P(),
            P(),
            P(),
            P(),
        ),
        out_specs=(P(("patch", "group"), None), P(("patch", "group"), None)),
        check_vma=False,
    )
```

profile of v0, /device:TPU:1, one launch (start us, length us, event | category | flops | bytes accessed | tf_op | source)
XLA Modules:
  0.0 108.4 jit_solution(11747875148235382991)
XLA Ops:
  7.2 0.0 copy-start
  7.2 0.0 copy-start.20
  7.2 0.0 reduce-scatter.2.cloned.1.call-start
  7.3 0.8 compare_select_fusion.4
  8.1 0.6 copy-done.13
  8.7 2.3 %gather_fusion = bf16[256,512]{1,0:T(8,128)(2,1)S(1)} fusion(bf16[512,512]{1,0:T(8,128)(2,1)} %param.20, s32[1024]{0:T(1024)S(1)} %pad_clamp_fusion.4), kind=kCustom, calls=%fused_computation | custom fusion | bytes 525312 | tf_op jit(solution)/shard_map/gather | solution.py:162
  11.0 2.6 %collective-permute-start = (bf16[128,512]{1,0:T(8,128)(2,1)S(1)}, bf16[128,512]{1,0:T(8,128)(2,1)S(1)}, u32[]{:S(2)}, u32[]{:S(2)}) collective-permute-start(bf16[128,512]{1,0:T(8,128)(2,1)S(1)} %get-tuple-element.20), channel_id=1, source_target_pairs={{0,4},{4,8},{8,12},{12,16},{16,20},{20,24},{24,28},{28,0},{1,5},{5... | collective-permute-start | bytes 393224 | tf_op jit(solution)/shard_map/ppermute | solution.py:16
  15.1 0.3 fusion.69
  15.5 3.1 %gather_fusion.2 = f32[768,512]{1,0:T(8,128)} fusion(f32[256,512]{1,0:T(8,128)S(1)} %fusion.69, s32[1024]{0:T(1024)S(1)} %pad_clamp_fusion.2), kind=kCustom, calls=%fused_computation.2 | custom fusion | bytes 3148800 | tf_op jit(solution)/shard_map/gather | solution.py:44
  18.6 0.0 collective-permute-done.1
  18.6 0.6 fusion.7
  19.2 3.1 %gather_fusion.1 = f32[768,512]{1,0:T(8,128)} fusion(f32[768,512]{1,0:T(8,128)S(1)} %fusion.7, s32[1024]{0:T(1024)S(1)} %pad_clamp_fusion.3), kind=kCustom, calls=%fused_computation.1 | custom fusion | bytes 3148800 | tf_op jit(solution)/shard_map/gather | solution.py:44
  22.3 2.9 %fusion.67 = (f32[256]{0:T(256)S(1)}, f32[256,512]{1,0:T(8,128)S(1)}) fusion(bf16[512,512]{1,0:T(8,128)(2,1)} %param.32, f32[768,512]{1,0:T(8,128)} %gather_fusion.1, f32[768,512]{1,0:T(8,128)} %gather_fusion.2, s32[768]{0:T(1024)S(1)} %copy-done.18, pred[768]{0:T(1024)(128)(4,1)S(1)} %iota_compare_fusion.9), kind=kOutput, calls=%fused_computation.111 | convolution fusion | flops 607256320 | bytes 4199168 | tf_op jit(solution)/shard_map/dot_general | solution.py:51
  25.2 0.2 multiply_reduce_fusion.2
  25.5 0.2 add_convert_fusion
  25.7 10.7 %all_gather.3 = bf16[64,512]{1,0:T(8,128)(2,1)S(1)} all-gather(bf16[16,512]{1,0:T(8,128)(2,1)S(1)} %slice.72), channel_id=1, replica_groups=mesh['patch'=8,'group'=4] {'group'}, dimensions={0}, use_global_device_ids=true | all-gather | bytes 81920 | tf_op jit(solution)/shard_map/all_gather | solution.py:178
  36.4 0.3 fusion.70
  36.7 0.2 fusion.71
  36.9 0.3 fusion.72
  37.3 3.1 %gather_fusion.3 = f32[768,512]{1,0:T(8,128)} fusion(f32[320,512]{1,0:T(8,128)S(1)} %pad_maximum_fusion, s32[1024]{0:T(1024)S(1)} %pad_clamp_fusion.1), kind=kCustom, calls=%fused_computation.3 | custom fusion | bytes 3148800 | tf_op jit(solution)/shard_map/gather | solution.py:44
  40.4 3.1 %gather_fusion.4 = f32[768,512]{1,0:T(8,128)} fusion(f32[256,512]{1,0:T(8,128)S(1)} %fusion.72, s32[1024]{0:T(1024)S(1)} %pad_clamp_fusion), kind=kCustom, calls=%fused_computation.4 | custom fusion | bytes 3148800 | tf_op jit(solution)/shard_map/gather | solution.py:44
  43.5 2.9 %fusion.68 = (f32[256]{0:T(256)S(1)}, f32[256,512]{1,0:T(8,128)S(1)}) fusion(bf16[512,512]{1,0:T(8,128)(2,1)} %param.36, f32[768,512]{1,0:T(8,128)} %gather_fusion.3, f32[768,512]{1,0:T(8,128)} %gather_fusion.4, s32[768]{0:T(1024)S(1)} %copy-done.10, pred[768]{0:T(1024)(128)(4,1)S(1)} %iota_compare_fusion.8), kind=kOutput, calls=%fused_computation.112 | convolution fusion | flops 607256320 | bytes 4199168 | tf_op jit(solution)/shard_map/dot_general | solution.py:51
  46.4 0.2 multiply_reduce_fusion.1
  46.7 0.2 fusion.31
  46.9 0.2 fusion.33
  47.1 3.3 %gather_fusion.5 = bf16[768,512]{1,0:T(8,128)(2,1)} fusion(bf16[256,512]{1,0:T(8,128)(2,1)S(1)} %fusion.33, s32[1024]{0:T(1024)S(1)} %pad_clamp_fusion), kind=kCustom, calls=%fused_computation.5 | custom fusion | bytes 1575936 | tf_op jit(solution)/shard_map/gather | solution.py:58
  50.5 3.2 %multiply_convert_fusion.1 = bf16[768,512]{1,0:T(8,128)(2,1)S(1)} fusion(bf16[512,512]{1,0:T(8,128)(2,1)} %param.36, bf16[768,512]{1,0:T(8,128)(2,1)} %gather_fusion.5, pred[768]{0:T(1024)(128)(4,1)S(1)} %iota_compare_fusion.8, f32[768,512]{1,0:T(8,128)} %gather_fusion.3, f32[768,512]{1,0:T(8,128)} %gather_fusion.4), kind=kOutput, calls=%fused_computation.12 | convolution fusion | flops 406978560 | bytes 5243648 | tf_op jit(solution)/shard_map/dot_general | solution.py:59
  53.7 0.9 copy-done.6
  54.6 0.4 fusion.6
  55.0 1.3 %fusion.54 = f32[64,512]{1,0:T(8,128)} fusion(bf16[512,512]{1,0:T(8,128)(2,1)S(1)} %copy-done.1, f32[320,512]{1,0:T(8,128)S(1)} %fusion.6), kind=kOutput, calls=%fused_computation.79 | convolution fusion | flops 201326592 | bytes 786432 | tf_op jit(solution)/shard_map/dot_general | solution.py:196
  56.3 0.3 convolution_add_fusion.2
  56.6 0.0 reduce-scatter.2.cloned.1.call-update
  56.6 1.7 %convolution_add_fusion.1 = f32[256,512]{1,0:T(8,128)S(1)} fusion(f32[256,512]{1,0:T(8,128)S(1)} %convolution_add_fusion.2, bf16[512,512]{1,0:T(8,128)(2,1)S(1)} %copy-done.4, bf16[768,512]{1,0:T(8,128)(2,1)} %copy-done.6, s32[768]{0:T(1024)S(1)} %copy-done.10, pred[768]{0:T(1024)(128)(4,1)} %copy-done.22), kind=kOutput, calls=%fused_computation.24 | convolution fusion | flops 336199680 | bytes 2363136 | tf_op jit(solution)/shard_map/dot_general | solution.py:134
  58.4 19.3 %reduce-scatter.2.cloned.1.call-done = f32[16,512]{1,0:T(8,128)} async-done(((f32[64,512]{1,0:T(8,128)}), f32[16,512]{1,0:T(8,128)}) %reduce-scatter.2.cloned.1.call-update) | async-done | bytes 32784 | tf_op jit(solution)/shard_map/reduce_scatter | solution.py:195
  77.7 0.8 fusion.56
  78.5 0.2 multiply_reduce_fusion.3
  78.7 0.2 subtract_multiply_fusion
  79.0 2.7 %gather_fusion.6 = bf16[768,512]{1,0:T(8,128)(2,1)S(1)} fusion(bf16[256,512]{1,0:T(8,128)(2,1)S(1)} %subtract_multiply_fusion, s32[1024]{0:T(1024)S(1)} %pad_clamp_fusion.2), kind=kCustom, calls=%fused_computation.6 | custom fusion | bytes 1575936 | tf_op jit(solution)/shard_map/gather | solution.py:58
  81.7 3.7 %multiply_convert_fusion = bf16[768,512]{1,0:T(8,128)(2,1)} fusion(bf16[512,512]{1,0:T(8,128)(2,1)S(1)} %copy-done.23, bf16[768,512]{1,0:T(8,128)(2,1)S(1)} %gather_fusion.6, pred[768]{0:T(1024)(128)(4,1)S(1)} %copy-done.25, f32[768,512]{1,0:T(8,128)} %gather_fusion.1, f32[768,512]{1,0:T(8,128)} %gather_fusion.2), kind=kOutput, calls=%fused_computation.10 | convolution fusion | flops 406978560 | bytes 5243648 | tf_op jit(solution)/shard_map/dot_general | solution.py:59
  85.5 2.5 %fusion.4 = bf16[256,512]{1,0:T(8,128)(2,1)} fusion(f32[256,512]{1,0:T(8,128)S(1)} %fusion.56, bf16[512,512]{1,0:T(8,128)(2,1)S(1)} %copy-done.8, bf16[768,512]{1,0:T(8,128)(2,1)} %multiply_convert_fusion, s32[768]{0:T(1024)S(1)} %copy-done.19, pred[768]{0:T(1024)(128)(4,1)S(1)} %copy-done.25), kind=kOutput, calls=%fused_computation.26 | convolution fusion | flops 336330752 | bytes 2100992 | tf_op jit(solution)/shard_map/dot_general | solution.py:98
  88.0 0.8 fusion.1
  88.8 4.1 %collective-permute-start.2 = (bf16[128,512]{1,0:T(8,128)(2,1)S(1)}, bf16[128,512]{1,0:T(8,128)(2,1)S(1)}, u32[]{:S(2)}, u32[]{:S(2)}) collective-permute-start(bf16[128,512]{1,0:T(8,128)(2,1)S(1)} %get-tuple-element.18), channel_id=1, source_target_pairs={{0,4},{4,8},{8,12},{12,16},{16,20},{20,24},{24,28},{28,0},{1,5},{5... | collective-permute-start | bytes 393224 | tf_op jit(solution)/shard_map/ppermute | solution.py:16
  92.9 0.5 fusion.35
  93.4 1.5 %collective-permute-done.2 = bf16[128,512]{1,0:T(8,128)(2,1)S(1)} collective-permute-done((bf16[128,512]{1,0:T(8,128)(2,1)S(1)}, bf16[128,512]{1,0:T(8,128)(2,1)S(1)}, u32[]{:S(2)}, u32[]{:S(2)}) %collective-permute-start.2) | collective-permute-done | bytes 131104 | tf_op jit(solution)/shard_map/ppermute | solution.py:16
  94.9 3.0 %collective-permute-done.3 = bf16[128,512]{1,0:T(8,128)(2,1)S(1)} collective-permute-done((bf16[128,512]{1,0:T(8,128)(2,1)S(1)}, bf16[128,512]{1,0:T(8,128)(2,1)S(1)}, u32[]{:S(2)}, u32[]{:S(2)}) %collective-permute-start.3) | collective-permute-done | bytes 131104 | tf_op jit(solution)/shard_map/ppermute | solution.py:17
  97.9 0.3 fusion.50
  98.2 2.5 %scatter_fusion = f32[512,512]{1,0:T(8,128)S(1)} fusion(f32[512,512]{1,0:T(8,128)S(1)} %fusion.35, s32[256]{0:T(256)S(1)} %copy-done.14, f32[256,512]{1,0:T(8,128)S(1)} %fusion.50), kind=kCustom, calls=%fused_computation.7 | custom fusion | flops 131072 | bytes 1573888 | tf_op jit(solution)/shard_map/scatter-add | solution.py:223
  100.7 0.9 convert_element_type.67
  (75 shorter events, 0.3 us)
Async XLA Ops:
  7.2 11.5 %copy-start = (bf16[512,512]{1,0:T(8,128)(2,1)S(1)}, bf16[512,512]{1,0:T(8,128)(2,1)}, u32[]{:S(2)}) copy-start(bf16[512,512]{1,0:T(8,128)(2,1)} %param.30) | copy-start | bytes 1572868
  7.2 7.8 %copy-start.20 = (s32[768]{0:T(1024)S(1)}, s32[768]{0:T(1024)}, u32[]{:S(2)}) copy-start(s32[768]{0:T(1024)} %param.24) | copy-start | bytes 9220
  7.2 7.8 %copy-start.16 = (s32[768]{0:T(1024)S(1)}, s32[768]{0:T(1024)}, u32[]{:S(2)}) copy-start(s32[768]{0:T(1024)} %param.27) | copy-start | bytes 9220
  7.2 7.9 %copy-start.18 = (s32[768]{0:T(1024)S(1)}, s32[768]{0:T(1024)}, u32[]{:S(2)}) copy-start(s32[768]{0:T(1024)} %param.25) | copy-start | bytes 9220
  7.2 7.9 %copy-start.10 = (s32[768]{0:T(1024)S(1)}, s32[768]{0:T(1024)}, u32[]{:S(2)}) copy-start(s32[768]{0:T(1024)} %param.28) | copy-start | bytes 9220
  7.2 7.9 %copy-start.7 = (bf16[512,512]{1,0:T(8,128)(2,1)S(1)}, bf16[512,512]{1,0:T(8,128)(2,1)}, u32[]{:S(2)}) copy-start(bf16[512,512]{1,0:T(8,128)(2,1)} %param.31) | copy-start | bytes 1572868
  7.2 7.9 %copy-start.5 = (bf16[256,512]{1,0:T(8,128)(2,1)S(1)}, bf16[256,512]{1,0:T(8,128)(2,1)}, u32[]{:S(2)}) copy-start(bf16[256,512]{1,0:T(8,128)(2,1)} %param.21) | copy-start | bytes 786436
  7.2 70.4 %reduce-scatter.2.cloned.1.call-start = ((), (), s32[]{:S(2)}) async-start(), calls=%async_computation.1 | async-start | bytes 163840 | tf_op jit(solution)/shard_map/reduce_scatter | solution.py:195
  8.1 0.6 copy-start.13
  11.0 7.6 %collective-permute-start = (bf16[128,512]{1,0:T(8,128)(2,1)S(1)}, bf16[128,512]{1,0:T(8,128)(2,1)S(1)}, u32[]{:S(2)}, u32[]{:S(2)}) collective-permute-start(bf16[128,512]{1,0:T(8,128)(2,1)S(1)} %get-tuple-element.20), channel_id=1, source_target_pairs={{0,4},{4,8},{8,12},{12,16},{16,20},{20,24},{24,28},{28,0},{1,5},{5... | collective-permute-start | bytes 393224 | tf_op jit(solution)/shard_map/ppermute | solution.py:16
  13.7 5.0 %collective-permute-start.1 = (bf16[128,512]{1,0:T(8,128)(2,1)S(1)}, bf16[128,512]{1,0:T(8,128)(2,1)S(1)}, u32[]{:S(2)}, u32[]{:S(2)}) collective-permute-start(bf16[128,512]{1,0:T(8,128)(2,1)S(1)} %get-tuple-element.21), channel_id=1, source_target_pairs={{4,0},{8,4},{12,8},{16,12},{20,16},{24,20},{28,24},{0,28},{5,1},{9... | collective-permute-start | bytes 393224 | tf_op jit(solution)/shard_map/ppermute | solution.py:17
  15.0 7.3 %copy-start.24 = (pred[768]{0:T(1024)(128)(4,1)}, pred[768]{0:T(1024)(128)(4,1)S(1)}, u32[]{:S(2)}) copy-start(pred[768]{0:T(1024)(128)(4,1)S(1)} %iota_compare_fusion.9) | copy-start | bytes 2308
  15.4 35.0 %copy-start.22 = (pred[768]{0:T(1024)(128)(4,1)}, pred[768]{0:T(1024)(128)(4,1)S(1)}, u32[]{:S(2)}) copy-start(pred[768]{0:T(1024)(128)(4,1)S(1)} %iota_compare_fusion.8) | copy-start | bytes 2308
  15.5 3.2 %copy-start.2 = (bf16[512,512]{1,0:T(8,128)(2,1)S(1)}, bf16[512,512]{1,0:T(8,128)(2,1)}, u32[]{:S(2)}) copy-start(bf16[512,512]{1,0:T(8,128)(2,1)} %param.20) | copy-start | bytes 1572868
  22.3 3.1 %copy-start.9 = (f32[512]{0:T(512)S(1)}, f32[512]{0:T(512)}, u32[]{:S(2)}) copy-start(f32[512]{0:T(512)} %param.33) | copy-start | bytes 6148
  25.2 11.2 %copy-start.1 = (bf16[512,512]{1,0:T(8,128)(2,1)S(1)}, bf16[512,512]{1,0:T(8,128)(2,1)}, u32[]{:S(2)}) copy-start(bf16[512,512]{1,0:T(8,128)(2,1)} %param.34) | copy-start | bytes 1572868
  25.4 11.5 %copy-start.11 = (f32[256]{0:T(256)}, f32[256]{0:T(256)S(1)}, u32[]{:S(2)}) copy-start(f32[256]{0:T(256)S(1)} %add_rsqrt_fusion.1) | copy-start | bytes 3076
  25.5 11.5 %copy-start.4 = (bf16[512,512]{1,0:T(8,128)(2,1)S(1)}, bf16[512,512]{1,0:T(8,128)(2,1)}, u32[]{:S(2)}) copy-start(bf16[512,512]{1,0:T(8,128)(2,1)} %param.35) | copy-start | bytes 1572868
  43.5 3.2 %copy-start.3 = (bf16[256,512]{1,0:T(8,128)(2,1)S(1)}, bf16[256,512]{1,0:T(8,128)(2,1)}, u32[]{:S(2)}) copy-start(bf16[256,512]{1,0:T(8,128)(2,1)} %param.22) | copy-start | bytes 786436
  43.5 3.2 %copy-start.15 = (f32[512]{0:T(512)S(1)}, f32[512]{0:T(512)}, u32[]{:S(2)}) copy-start(f32[512]{0:T(512)} %param.37) | copy-start | bytes 6148
  50.5 4.1 %copy-start.17 = (s32[768]{0:T(1024)S(1)}, s32[768]{0:T(1024)}, u32[]{:S(2)}) copy-start(s32[768]{0:T(1024)} %param.27) | copy-start | bytes 9220
  53.7 0.9 copy-start.6
  56.6 21.9 %copy-start.12 = (f32[256]{0:T(256)S(1)}, f32[256]{0:T(256)}, u32[]{:S(2)}) copy-start(f32[256]{0:T(256)} %copy-done.11) | copy-start | bytes 3076
  78.9 2.7 %copy-start.23 = (bf16[512,512]{1,0:T(8,128)(2,1)S(1)}, bf16[512,512]{1,0:T(8,128)(2,1)}, u32[]{:S(2)}) copy-start(bf16[512,512]{1,0:T(8,128)(2,1)} %param.32) | copy-start | bytes 1572868
  79.0 2.7 %copy-start.25 = (pred[768]{0:T(1024)(128)(4,1)S(1)}, pred[768]{0:T(1024)(128)(4,1)}, u32[]{:S(2)}) copy-start(pred[768]{0:T(1024)(128)(4,1)} %copy-done.24) | copy-start | bytes 2308
  81.7 3.8 %copy-start.8 = (bf16[512,512]{1,0:T(8,128)(2,1)S(1)}, bf16[512,512]{1,0:T(8,128)(2,1)}, u32[]{:S(2)}) copy-start(bf16[512,512]{1,0:T(8,128)(2,1)} %param.31) | copy-start | bytes 1572868
  81.7 3.8 %copy-start.19 = (s32[768]{0:T(1024)S(1)}, s32[768]{0:T(1024)}, u32[]{:S(2)}) copy-start(s32[768]{0:T(1024)} %param.25) | copy-start | bytes 9220
  85.5 2.5 %copy-start.21 = (s32[768]{0:T(1024)S(1)}, s32[768]{0:T(1024)}, u32[]{:S(2)}) copy-start(s32[768]{0:T(1024)} %param.24) | copy-start | bytes 9220
  85.5 2.5 %copy-start.26 = (bf16[768,512]{1,0:T(8,128)(2,1)S(1)}, bf16[768,512]{1,0:T(8,128)(2,1)}, u32[]{:S(2)}) copy-start(bf16[768,512]{1,0:T(8,128)(2,1)} %multiply_convert_fusion) | copy-start | bytes 2359300
  88.8 6.1 %collective-permute-start.2 = (bf16[128,512]{1,0:T(8,128)(2,1)S(1)}, bf16[128,512]{1,0:T(8,128)(2,1)S(1)}, u32[]{:S(2)}, u32[]{:S(2)}) collective-permute-start(bf16[128,512]{1,0:T(8,128)(2,1)S(1)} %get-tuple-element.18), channel_id=1, source_target_pairs={{0,4},{4,8},{8,12},{12,16},{16,20},{20,24},{24,28},{28,0},{1,5},{5... | collective-permute-start | bytes 393224 | tf_op jit(solution)/shard_map/ppermute | solution.py:16
  92.9 5.3 %copy-start.14 = (s32[256]{0:T(256)S(1)}, s32[256]{0:T(256)}, u32[]{:S(2)}) copy-start(s32[256]{0:T(256)} %copy-done.13) | copy-start | bytes 3076
  92.9 4.9 %collective-permute-start.3 = (bf16[128,512]{1,0:T(8,128)(2,1)S(1)}, bf16[128,512]{1,0:T(8,128)(2,1)S(1)}, u32[]{:S(2)}, u32[]{:S(2)}) collective-permute-start(bf16[128,512]{1,0:T(8,128)(2,1)S(1)} %get-tuple-element.19), channel_id=1, source_target_pairs={{4,0},{8,4},{12,8},{16,12},{20,16},{24,20},{28,24},{0,28},{5,1},{9... | collective-permute-start | bytes 393224 | tf_op jit(solution)/shard_map/ppermute | solution.py:17
Sparse Core Ops, SparseCore 0:
  56.8 20.8 reduce-scatter.1
where the time goes:
time: 109 us; the launch traced here: 108 us
  waiting for transfers between devices  23.8 us (22%)
  local copies, waits for them, and re-layouts  22.4 us (21%)
  matrix products  22.2 us (20%)
  between operations  15.9 us (15%)
  blocking collectives  10.7 us (10%)
  starting transfers between devices  6.83 us (6%)
  other arithmetic  6.52 us (6%)
    reduce_scatter x1, waiting for transfers between devices, on_device(): lax.psum_scatter(jnp.dot(grad_coarse, back_weight, precision=lax.Precisio...  19.3 us
    gather x4, local copies, waits for them, and re-layouts, edge_forward(): preact = source[sender] + dest_proj[target]  12.5 us
    all_gather x1, blocking collectives, on_device(): lax.all_gather(updated[:coarse_rows], 'group', axis=0, tiled=True)  10.7 us
    dot_general x2, matrix products, edge_backward(): jnp.dot(grad_message, out_weight.T, preferred_element_type=jnp.float32)  6.96 us
    ppermute x2, starting transfers between devices, padded_2(): before = lax.ppermute(last, axis, up)  6.78 us
    gather x2, local copies, waits for them, and re-layouts, edge_backward(): grad_gathered[target]  6 us
    dot_general x2, matrix products, edge_forward(): gathered = jnp.dot(onehot, message, preferred_element_type=jnp.float32)  5.79 us
    ppermute x2, waiting for transfers between devices, padded_2(): after = lax.ppermute(initial, axis, down)  3.03 us
  transfers between devices with their start and end apart: 5, of which 3 were waited for; matrix products, arithmetic and copies ran while one was open for 5% of the time, Pallas kernels for 0%

commit v1 on v0

--- a/solution.py
+++ b/solution.py
@@ -4,6 +4,18 @@
 from jax.sharding import PartitionSpec as P
 
 EPSILON = 1e-05
+
+
+def gather_by_bits(x, axis, dim):
+    ways, here, step = (lax.axis_size(axis), lax.axis_index(axis), x.shape[dim])
+    line, have = (x, 1)
+    while have < ways:
+        line = jnp.concatenate(
+            [line, lax.ppermute(line, axis, [(d, (d - have) % ways) for d in range(ways)])],
+            axis=dim,
+        )
+        have = 2 * have
+    return jnp.roll(line, here * step, axis=dim)
 
 
 def padded_2(x, sides, width):
@@ -175,7 +187,7 @@
     )
     coarse_rows = mesh_latent.shape[0] // 16
     coarse_proj = jnp.dot(
-        lax.all_gather(updated[:coarse_rows], "group", axis=0, tiled=True),
+        gather_by_bits(updated[:coarse_rows], "group", 0),
         process_source,
         preferred_element_type=jnp.float32,
     )

time: 109 us -> 108 us (level)
  blocking collectives: 10.7 us -> 0 us
  local copies, waits for them, and re-layouts: 22.4 us -> 26.4 us
  starting transfers between devices: 6.83 us -> 10.2 us
  matrix products: 22.2 us -> 23.8 us
  other arithmetic: 6.52 us -> 7.66 us
    all_gather x1 -> x0, blocking collectives: 10.7 us -> none  [on_device(): lax.all_gather(updated[:coarse_rows], 'group', axis=0, tiled=True)]
    ppermute x0 -> x2, starting transfers between devices: none -> 3.39 us  [gather_by_bits(): lax.ppermute(line, axis, [(d, (d - have) % ways) for d in range(ways)])]
    ppermute x0 -> x2, waiting for transfers between devices: none -> 3.04 us  [gather_by_bits(): lax.ppermute(line, axis, [(d, (d - have) % ways) for d in range(ways)])]
    reduce_scatter x1, waiting for transfers between devices: 19.3 us -> 16.3 us  [on_device(): lax.psum_scatter(jnp.dot(grad_coarse, back_weight, precision=lax.Precisio...]
    unnamed x54 -> x66, local copies, waits for them, and re-layouts: 1.59 us -> 4.14 us
  transfers between devices with their start and end apart: 5 -> 7, of which waited for: 3 -> 4; matrix products, arithmetic and copies ran while one was open for 5% -> 10% of each run, Pallas kernels for 0% -> 0%
where the time goes in v1:
time: 108 us
  local copies, waits for them, and re-layouts  26.4 us (24%)
  matrix products  23.8 us (22%)
  waiting for transfers between devices  23.8 us (22%)
  between operations  15.9 us (15%)
  starting transfers between devices  10.2 us (9%)
  other arithmetic  7.66 us (7%)
    reduce_scatter x1, waiting for transfers between devices, on_device(): lax.psum_scatter(jnp.dot(grad_coarse, back_weight, precision=lax.Precisio...  16.3 us
    gather x4, local copies, waits for them, and re-layouts, edge_forward(): preact = source[sender] + dest_proj[target]  12.6 us
    dot_general x2, matrix products, edge_backward(): jnp.dot(grad_message, out_weight.T, preferred_element_type=jnp.float32)  6.8 us
    ppermute x2, starting transfers between devices, padded_2(): before = lax.ppermute(last, axis, up)  6.76 us
    gather x2, local copies, waits for them, and re-layouts, edge_backward(): grad_gathered[target]  6.02 us
    dot_general x2, matrix products, edge_forward(): gathered = jnp.dot(onehot, message, preferred_element_type=jnp.float32)  5.71 us
    unnamed x66, local copies, waits for them, and re-layouts  4.14 us
    ppermute x2, starting transfers between devices, gather_by_bits(): lax.ppermute(line, axis, [(d, (d - have) % ways) for d in range(ways)])  3.39 us
  transfers between devices with their start and end apart: 7, of which 4 were waited for; matrix products, arithmetic and copies ran while one was open for 10% of the time, Pallas kernels for 0%

profile of v1, /device:TPU:1, one launch (start us, length us, event | category | flops | bytes accessed | tf_op | source)
XLA Modules:
  0.0 107.8 jit_solution(4593766827617686264)
XLA Ops:
  7.3 0.8 compare_select_fusion.4
  8.1 2.3 %gather_fusion = bf16[256,512]{1,0:T(8,128)(2,1)S(1)} fusion(bf16[512,512]{1,0:T(8,128)(2,1)} %param.20, s32[1024]{0:T(1024)S(1)} %pad_clamp_fusion.4), kind=kCustom, calls=%fused_computation | custom fusion | bytes 525312 | tf_op jit(solution)/shard_map/gather | solution.py:174
  10.4 2.6 %collective-permute-start = (bf16[128,512]{1,0:T(8,128)(2,1)S(1)}, bf16[128,512]{1,0:T(8,128)(2,1)S(1)}, u32[]{:S(2)}, u32[]{:S(2)}) collective-permute-start(bf16[128,512]{1,0:T(8,128)(2,1)S(1)} %get-tuple-element.22), channel_id=1, source_target_pairs={{0,4},{4,8},{8,12},{12,16},{16,20},{20,24},{24,28},{28,0},{1,5},{5... | collective-permute-start | bytes 393224 | tf_op jit(solution)/shard_map/ppermute | solution.py:28
  14.5 0.3 fusion.73
  14.8 0.6 iota_compare_fusion.8
  15.4 3.1 %gather_fusion.2 = f32[768,512]{1,0:T(8,128)} fusion(f32[256,512]{1,0:T(8,128)S(1)} %fusion.73, s32[1024]{0:T(1024)S(1)} %get-tuple-element.30), kind=kCustom, calls=%fused_computation.2 | custom fusion | bytes 3148800 | tf_op jit(solution)/shard_map/gather | solution.py:56
  18.5 0.6 pad_clamp_fusion
  19.1 0.7 copy-done.27
  19.8 1.5 %fusion.7 = f32[768,512]{1,0:T(8,128)S(1)} fusion(bf16[512,512]{1,0:T(8,128)(2,1)S(1)} %copy-done, bf16[128,512]{1,0:T(8,128)(2,1)} %collective-permute-done.1, bf16[128,512]{1,0:T(8,128)(2,1)} %copy-done.27, bf16[512,512]{1,0:T(8,128)(2,1)S(1)} %copy-done.2), kind=kOutput, calls=%fused_computation.32 | convolution fusion | flops 405012480 | bytes 2883584 | tf_op jit(solution)/shard_map/dot_general | solution.py:92
  21.4 3.1 %gather_fusion.1 = f32[768,512]{1,0:T(8,128)} fusion(f32[768,512]{1,0:T(8,128)S(1)} %fusion.7, s32[1024]{0:T(1024)S(1)} %get-tuple-element.31), kind=kCustom, calls=%fused_computation.1 | custom fusion | bytes 3148800 | tf_op jit(solution)/shard_map/gather | solution.py:56
  24.5 2.8 %fusion.71 = (f32[256]{0:T(256)S(1)}, f32[256,512]{1,0:T(8,128)S(1)}) fusion(bf16[512,512]{1,0:T(8,128)(2,1)S(1)} %copy-done.25, f32[768,512]{1,0:T(8,128)} %gather_fusion.1, f32[768,512]{1,0:T(8,128)} %gather_fusion.2, s32[768]{0:T(1024)S(1)} %copy-done.19, pred[768]{0:T(1024)(128)(4,1)S(1)} %iota_compare_fusion.9), kind=kOutput, calls=%fused_computation.122 | convolution fusion | flops 607256320 | bytes 4199168 | tf_op jit(solution)/shard_map/dot_general | solution.py:63
  27.7 0.6 fusion.69
  28.3 3.3 %collective-permute-start.2 = (bf16[16,512]{1,0:T(8,128)(2,1)S(1)}, bf16[16,512]{1,0:T(8,128)(2,1)S(1)}, u32[]{:S(2)}, u32[]{:S(2)}) collective-permute-start(bf16[16,512]{1,0:T(8,128)(2,1)S(1)} %get-tuple-element.20), channel_id=1, source_target_pairs={{0,3},{1,0},{2,1},{3,2},{4,7},{5,4},{6,5},{7,6},{8,11},{9,8},{10,9... | collective-permute-start | bytes 49160 | tf_op jit(solution)/shard_map/ppermute | solution.py:14
  31.7 0.3 fusion.75
  32.0 0.3 fusion.74
  32.3 3.1 %gather_fusion.4 = f32[768,512]{1,0:T(8,128)} fusion(f32[256,512]{1,0:T(8,128)S(1)} %fusion.75, s32[1024]{0:T(1024)S(1)} %get-tuple-element.28), kind=kCustom, calls=%fused_computation.4 | custom fusion | bytes 3148800 | tf_op jit(solution)/shard_map/gather | solution.py:56
  35.5 0.6 constant_dynamic-update-slice_fusion.4
  36.1 3.0 %collective-permute-done.3 = bf16[32,512]{1,0:T(8,128)(2,1)S(1)} collective-permute-done((bf16[32,512]{1,0:T(8,128)(2,1)S(1)}, bf16[32,512]{1,0:T(8,128)(2,1)S(1)}, u32[]{:S(2)}, u32[]{:S(2)}) %collective-permute-start.3) | collective-permute-done | bytes 32800 | tf_op jit(solution)/shard_map/ppermute | solution.py:14
  39.1 0.6 constant_dynamic-update-slice_fusion.3
  39.8 0.6 constant_dynamic-update-slice_fusion.2
  40.4 0.6 constant_dynamic-update-slice_fusion.1
  41.0 0.6 constant_dynamic-update-slice_fusion
  41.6 1.0 fusion.56
  42.7 3.2 %gather_fusion.3 = f32[768,512]{1,0:T(8,128)} fusion(f32[320,512]{1,0:T(8,128)S(1)} %pad_maximum_fusion, s32[1024]{0:T(1024)} %get-tuple-element.29), kind=kCustom, calls=%fused_computation.3 | custom fusion | bytes 3148800 | tf_op jit(solution)/shard_map/gather | solution.py:56
  45.9 2.9 %fusion.72 = (f32[256]{0:T(256)S(1)}, f32[256,512]{1,0:T(8,128)S(1)}) fusion(bf16[512,512]{1,0:T(8,128)(2,1)} %param.36, f32[768,512]{1,0:T(8,128)} %gather_fusion.3, f32[768,512]{1,0:T(8,128)} %gather_fusion.4, s32[768]{0:T(1024)} %param.28, pred[768]{0:T(1024)(128)(4,1)} %iota_compare_fusion.8), kind=kOutput, calls=%fused_computation.123 | convolution fusion | flops 607256320 | bytes 4199168 | tf_op jit(solution)/shard_map/dot_general | solution.py:63
  49.1 0.2 fusion.31
  49.6 3.3 %gather_fusion.5 = bf16[768,512]{1,0:T(8,128)(2,1)} fusion(bf16[256,512]{1,0:T(8,128)(2,1)S(1)} %fusion.33, s32[1024]{0:T(1024)S(1)} %get-tuple-element.28), kind=kCustom, calls=%fused_computation.5 | custom fusion | bytes 1575936 | tf_op jit(solution)/shard_map/gather | solution.py:70
  53.0 3.0 %multiply_convert_fusion.1 = bf16[768,512]{1,0:T(8,128)(2,1)S(1)} fusion(bf16[512,512]{1,0:T(8,128)(2,1)S(1)} %copy-done.24, bf16[768,512]{1,0:T(8,128)(2,1)} %gather_fusion.5, pred[768]{0:T(1024)(128)(4,1)S(1)} %copy-done.23, f32[768,512]{1,0:T(8,128)} %gather_fusion.3, f32[768,512]{1,0:T(8,128)} %gather_fusion.4), kind=kOutput, calls=%fused_computation.12 | convolution fusion | flops 406978560 | bytes 5243648 | tf_op jit(solution)/shard_map/dot_general | solution.py:71
  56.0 0.9 copy-done.6
  56.9 0.4 fusion.6
  57.4 1.3 %fusion.54 = f32[64,512]{1,0:T(8,128)} fusion(bf16[512,512]{1,0:T(8,128)(2,1)S(1)} %copy-done.1, f32[320,512]{1,0:T(8,128)S(1)} %fusion.6), kind=kOutput, calls=%fused_computation.79 | convolution fusion | flops 201326592 | bytes 786432 | tf_op jit(solution)/shard_map/dot_general | solution.py:208
  58.6 0.3 convolution_add_fusion.2
  59.0 1.7 %convolution_add_fusion.1 = f32[256,512]{1,0:T(8,128)S(1)} fusion(f32[256,512]{1,0:T(8,128)S(1)} %convolution_add_fusion.2, bf16[512,512]{1,0:T(8,128)(2,1)S(1)} %copy-done.4, bf16[768,512]{1,0:T(8,128)(2,1)} %copy-done.6, s32[768]{0:T(1024)S(1)} %copy-done.11, pred[768]{0:T(1024)(128)(4,1)} %iota_compare_fusion.8), kind=kOutput, calls=%fused_computation.24 | convolution fusion | flops 336199680 | bytes 2363136 | tf_op jit(solution)/shard_map/dot_general | solution.py:146
  60.7 16.3 %reduce-scatter.2.cloned.1.call-done = f32[16,512]{1,0:T(8,128)} async-done(((f32[64,512]{1,0:T(8,128)}), f32[16,512]{1,0:T(8,128)}) %reduce-scatter.2.cloned.1.call-update) | async-done | bytes 32784 | tf_op jit(solution)/shard_map/reduce_scatter | solution.py:207
  77.0 0.8 fusion.58
  77.8 0.2 multiply_reduce_fusion.3
  78.1 0.2 subtract_multiply_fusion
  78.3 2.7 %gather_fusion.6 = bf16[768,512]{1,0:T(8,128)(2,1)S(1)} fusion(bf16[256,512]{1,0:T(8,128)(2,1)S(1)} %subtract_multiply_fusion, s32[1024]{0:T(1024)S(1)} %get-tuple-element.30), kind=kCustom, calls=%fused_computation.6 | custom fusion | bytes 1575936 | tf_op jit(solution)/shard_map/gather | solution.py:70
  81.0 3.8 %multiply_convert_fusion = bf16[768,512]{1,0:T(8,128)(2,1)} fusion(bf16[512,512]{1,0:T(8,128)(2,1)S(1)} %copy-done.26, bf16[768,512]{1,0:T(8,128)(2,1)S(1)} %gather_fusion.6, pred[768]{0:T(1024)(128)(4,1)S(1)} %copy-done.29, f32[768,512]{1,0:T(8,128)} %gather_fusion.1, f32[768,512]{1,0:T(8,128)} %gather_fusion.2), kind=kOutput, calls=%fused_computation.10 | convolution fusion | flops 406978560 | bytes 5243648 | tf_op jit(solution)/shard_map/dot_general | solution.py:71
  84.8 2.5 %fusion.4 = bf16[256,512]{1,0:T(8,128)(2,1)} fusion(f32[256,512]{1,0:T(8,128)S(1)} %fusion.58, bf16[512,512]{1,0:T(8,128)(2,1)S(1)} %copy-done.8, bf16[768,512]{1,0:T(8,128)(2,1)} %multiply_convert_fusion, s32[768]{0:T(1024)S(1)} %copy-done.20, pred[768]{0:T(1024)(128)(4,1)S(1)} %copy-done.29), kind=kOutput, calls=%fused_computation.26 | convolution fusion | flops 336330752 | bytes 2100992 | tf_op jit(solution)/shard_map/dot_general | solution.py:110
  87.3 0.8 fusion.1
  88.1 4.1 %collective-permute-start.4 = (bf16[128,512]{1,0:T(8,128)(2,1)S(1)}, bf16[128,512]{1,0:T(8,128)(2,1)S(1)}, u32[]{:S(2)}, u32[]{:S(2)}) collective-permute-start(bf16[128,512]{1,0:T(8,128)(2,1)S(1)} %get-tuple-element.18), channel_id=1, source_target_pairs={{0,4},{4,8},{8,12},{12,16},{16,20},{20,24},{24,28},{28,0},{1,5},{5... | collective-permute-start | bytes 393224 | tf_op jit(solution)/shard_map/ppermute | solution.py:28
  92.3 0.5 fusion.35
  92.7 1.5 %collective-permute-done.4 = bf16[128,512]{1,0:T(8,128)(2,1)S(1)} collective-permute-done((bf16[128,512]{1,0:T(8,128)(2,1)S(1)}, bf16[128,512]{1,0:T(8,128)(2,1)S(1)}, u32[]{:S(2)}, u32[]{:S(2)}) %collective-permute-start.4) | collective-permute-done | bytes 131104 | tf_op jit(solution)/shard_map/ppermute | solution.py:28
  94.2 3.0 %collective-permute-done.5 = bf16[128,512]{1,0:T(8,128)(2,1)S(1)} collective-permute-done((bf16[128,512]{1,0:T(8,128)(2,1)S(1)}, bf16[128,512]{1,0:T(8,128)(2,1)S(1)}, u32[]{:S(2)}, u32[]{:S(2)}) %collective-permute-start.5) | collective-permute-done | bytes 131104 | tf_op jit(solution)/shard_map/ppermute | solution.py:29
  97.2 0.3 fusion.50
  97.6 2.5 %scatter_fusion = f32[512,512]{1,0:T(8,128)S(1)} fusion(f32[512,512]{1,0:T(8,128)S(1)} %fusion.35, s32[256]{0:T(256)S(1)} %copy-done.15, f32[256,512]{1,0:T(8,128)S(1)} %fusion.50), kind=kCustom, calls=%fused_computation.7 | custom fusion | flops 131072 | bytes 1573888 | tf_op jit(solution)/shard_map/scatter-add | solution.py:235
  100.1 0.9 convert_element_type.67
  (91 shorter events, 1.2 us)
Async XLA Ops:
  7.2 12.6 %copy-start = (bf16[512,512]{1,0:T(8,128)(2,1)S(1)}, bf16[512,512]{1,0:T(8,128)(2,1)}, u32[]{:S(2)}) copy-start(bf16[512,512]{1,0:T(8,128)(2,1)} %param.30) | copy-start | bytes 1572868
  7.2 7.2 %copy-start.21 = (s32[768]{0:T(1024)S(1)}, s32[768]{0:T(1024)}, u32[]{:S(2)}) copy-start(s32[768]{0:T(1024)} %param.24) | copy-start | bytes 9220
  7.2 7.2 %copy-start.17 = (s32[768]{0:T(1024)S(1)}, s32[768]{0:T(1024)}, u32[]{:S(2)}) copy-start(s32[768]{0:T(1024)} %param.27) | copy-start | bytes 9220
  7.2 7.3 %copy-start.19 = (s32[768]{0:T(1024)S(1)}, s32[768]{0:T(1024)}, u32[]{:S(2)}) copy-start(s32[768]{0:T(1024)} %param.25) | copy-start | bytes 9220
  7.2 7.3 %copy-start.10 = (s32[768]{0:T(1024)S(1)}, s32[768]{0:T(1024)}, u32[]{:S(2)}) copy-start(s32[768]{0:T(1024)} %param.28) | copy-start | bytes 9220
  7.2 7.3 %copy-start.7 = (bf16[512,512]{1,0:T(8,128)(2,1)S(1)}, bf16[512,512]{1,0:T(8,128)(2,1)}, u32[]{:S(2)}) copy-start(bf16[512,512]{1,0:T(8,128)(2,1)} %param.31) | copy-start | bytes 1572868
  7.2 7.3 %copy-start.5 = (bf16[256,512]{1,0:T(8,128)(2,1)S(1)}, bf16[256,512]{1,0:T(8,128)(2,1)}, u32[]{:S(2)}) copy-start(bf16[256,512]{1,0:T(8,128)(2,1)} %param.21) | copy-start | bytes 786436
  7.2 69.8 %reduce-scatter.2.cloned.1.call-start = ((), (), s32[]{:S(2)}) async-start(), calls=%async_computation.1 | async-start | bytes 163840 | tf_op jit(solution)/shard_map/reduce_scatter | solution.py:207
  8.1 6.4 %copy-start.14 = (s32[256]{0:T(256)}, s32[256]{0:T(256)S(1)}, u32[]{:S(2)}) copy-start(s32[256]{0:T(256)S(1)} %compare_select_fusion.4) | copy-start | bytes 3076
  10.4 8.7 %collective-permute-start = (bf16[128,512]{1,0:T(8,128)(2,1)S(1)}, bf16[128,512]{1,0:T(8,128)(2,1)S(1)}, u32[]{:S(2)}, u32[]{:S(2)}) collective-permute-start(bf16[128,512]{1,0:T(8,128)(2,1)S(1)} %get-tuple-element.22), channel_id=1, source_target_pairs={{0,4},{4,8},{8,12},{12,16},{16,20},{20,24},{24,28},{28,0},{1,5},{5... | collective-permute-start | bytes 393224 | tf_op jit(solution)/shard_map/ppermute | solution.py:28
  13.1 6.7 %collective-permute-start.1 = (bf16[128,512]{1,0:T(8,128)(2,1)S(1)}, bf16[128,512]{1,0:T(8,128)(2,1)}, u32[]{:S(2)}, u32[]{:S(2)}) collective-permute-start(bf16[128,512]{1,0:T(8,128)(2,1)S(1)} %get-tuple-element.23), channel_id=1, source_target_pairs={{4,0},{8,4},{12,8},{16,12},{20,16},{24,20},{28,24},{0,28},{5,1},{9... | collective-permute-start | bytes 393224 | tf_op jit(solution)/shard_map/ppermute | solution.py:29
  14.4 10.1 %copy-start.28 = (pred[768]{0:T(1024)(128)(4,1)}, pred[768]{0:T(1024)(128)(4,1)S(1)}, u32[]{:S(2)}) copy-start(pred[768]{0:T(1024)(128)(4,1)S(1)} %iota_compare_fusion.9) | copy-start | bytes 2308
  15.4 4.4 %copy-start.2 = (bf16[512,512]{1,0:T(8,128)(2,1)S(1)}, bf16[512,512]{1,0:T(8,128)(2,1)}, u32[]{:S(2)}) copy-start(bf16[512,512]{1,0:T(8,128)(2,1)} %param.20) | copy-start | bytes 1572868
  19.1 0.7 copy-start.27
  21.3 3.2 %copy-start.25 = (bf16[512,512]{1,0:T(8,128)(2,1)S(1)}, bf16[512,512]{1,0:T(8,128)(2,1)}, u32[]{:S(2)}) copy-start(bf16[512,512]{1,0:T(8,128)(2,1)} %param.32) | copy-start | bytes 1572868
  24.5 3.0 %copy-start.9 = (f32[512]{0:T(512)S(1)}, f32[512]{0:T(512)}, u32[]{:S(2)}) copy-start(f32[512]{0:T(512)} %param.33) | copy-start | bytes 6148
  27.3 4.4 %copy-start.4 = (bf16[512,512]{1,0:T(8,128)(2,1)S(1)}, bf16[512,512]{1,0:T(8,128)(2,1)}, u32[]{:S(2)}) copy-start(bf16[512,512]{1,0:T(8,128)(2,1)} %param.35) | copy-start | bytes 1572868
  27.3 4.7 %copy-start.1 = (bf16[512,512]{1,0:T(8,128)(2,1)S(1)}, bf16[512,512]{1,0:T(8,128)(2,1)}, u32[]{:S(2)}) copy-start(bf16[512,512]{1,0:T(8,128)(2,1)} %param.34) | copy-start | bytes 1572868
  27.5 0.8 copy-start.12
  28.3 7.1 %collective-permute-start.2 = (bf16[16,512]{1,0:T(8,128)(2,1)S(1)}, bf16[16,512]{1,0:T(8,128)(2,1)S(1)}, u32[]{:S(2)}, u32[]{:S(2)}) collective-permute-start(bf16[16,512]{1,0:T(8,128)(2,1)S(1)} %get-tuple-element.20), channel_id=1, source_target_pairs={{0,3},{1,0},{2,1},{3,2},{4,7},{5,4},{6,5},{7,6},{8,11},{9,8},{10,9... | collective-permute-start | bytes 49160 | tf_op jit(solution)/shard_map/ppermute | solution.py:14
  35.4 3.7 %collective-permute-start.3 = (bf16[32,512]{1,0:T(8,128)(2,1)S(1)}, bf16[32,512]{1,0:T(8,128)(2,1)S(1)}, u32[]{:S(2)}, u32[]{:S(2)}) collective-permute-start(bf16[32,512]{1,0:T(8,128)(2,1)S(1)} %pad_maximum_fusion.1), channel_id=1, source_target_pairs={{0,2},{1,3},{2,0},{3,1},{4,6},{5,7},{6,4},{7,5},{8,10},{9,11},{10,... | collective-permute-start | bytes 98312 | tf_op jit(solution)/shard_map/ppermute | solution.py:14
  45.9 3.2 %copy-start.3 = (bf16[256,512]{1,0:T(8,128)(2,1)S(1)}, bf16[256,512]{1,0:T(8,128)(2,1)}, u32[]{:S(2)}) copy-start(bf16[256,512]{1,0:T(8,128)(2,1)} %param.22) | copy-start | bytes 786436
  45.9 3.2 %copy-start.16 = (f32[512]{0:T(512)S(1)}, f32[512]{0:T(512)}, u32[]{:S(2)}) copy-start(f32[512]{0:T(512)} %param.37) | copy-start | bytes 6148
  49.6 3.4 %copy-start.23 = (pred[768]{0:T(1024)(128)(4,1)S(1)}, pred[768]{0:T(1024)(128)(4,1)}, u32[]{:S(2)}) copy-start(pred[768]{0:T(1024)(128)(4,1)} %iota_compare_fusion.8) | copy-start | bytes 2308
  49.6 3.4 %copy-start.24 = (bf16[512,512]{1,0:T(8,128)(2,1)S(1)}, bf16[512,512]{1,0:T(8,128)(2,1)}, u32[]{:S(2)}) copy-start(bf16[512,512]{1,0:T(8,128)(2,1)} %param.36) | copy-start | bytes 1572868
  53.0 4.0 %copy-start.18 = (s32[768]{0:T(1024)S(1)}, s32[768]{0:T(1024)}, u32[]{:S(2)}) copy-start(s32[768]{0:T(1024)} %param.27) | copy-start | bytes 9220
  56.0 0.9 copy-start.6
  57.3 1.6 %copy-start.11 = (s32[768]{0:T(1024)S(1)}, s32[768]{0:T(1024)}, u32[]{:S(2)}) copy-start(s32[768]{0:T(1024)} %param.28) | copy-start | bytes 9220
  59.0 18.8 %copy-start.13 = (f32[256]{0:T(256)S(1)}, f32[256]{0:T(256)}, u32[]{:S(2)}) copy-start(f32[256]{0:T(256)} %copy-done.12) | copy-start | bytes 3076
  78.3 2.7 %copy-start.26 = (bf16[512,512]{1,0:T(8,128)(2,1)S(1)}, bf16[512,512]{1,0:T(8,128)(2,1)}, u32[]{:S(2)}) copy-start(bf16[512,512]{1,0:T(8,128)(2,1)} %param.32) | copy-start | bytes 1572868
  78.3 2.7 %copy-start.29 = (pred[768]{0:T(1024)(128)(4,1)S(1)}, pred[768]{0:T(1024)(128)(4,1)}, u32[]{:S(2)}) copy-start(pred[768]{0:T(1024)(128)(4,1)} %copy-done.28) | copy-start | bytes 2308
  81.0 3.8 %copy-start.8 = (bf16[512,512]{1,0:T(8,128)(2,1)S(1)}, bf16[512,512]{1,0:T(8,128)(2,1)}, u32[]{:S(2)}) copy-start(bf16[512,512]{1,0:T(8,128)(2,1)} %param.31) | copy-start | bytes 1572868
  81.0 3.8 %copy-start.20 = (s32[768]{0:T(1024)S(1)}, s32[768]{0:T(1024)}, u32[]{:S(2)}) copy-start(s32[768]{0:T(1024)} %param.25) | copy-start | bytes 9220
  84.8 2.5 %copy-start.22 = (s32[768]{0:T(1024)S(1)}, s32[768]{0:T(1024)}, u32[]{:S(2)}) copy-start(s32[768]{0:T(1024)} %param.24) | copy-start | bytes 9220
  84.8 2.5 %copy-start.30 = (bf16[768,512]{1,0:T(8,128)(2,1)S(1)}, bf16[768,512]{1,0:T(8,128)(2,1)}, u32[]{:S(2)}) copy-start(bf16[768,512]{1,0:T(8,128)(2,1)} %multiply_convert_fusion) | copy-start | bytes 2359300
  88.1 6.1 %collective-permute-start.4 = (bf16[128,512]{1,0:T(8,128)(2,1)S(1)}, bf16[128,512]{1,0:T(8,128)(2,1)S(1)}, u32[]{:S(2)}, u32[]{:S(2)}) collective-permute-start(bf16[128,512]{1,0:T(8,128)(2,1)S(1)} %get-tuple-element.18), channel_id=1, source_target_pairs={{0,4},{4,8},{8,12},{12,16},{16,20},{20,24},{24,28},{28,0},{1,5},{5... | collective-permute-start | bytes 393224 | tf_op jit(solution)/shard_map/ppermute | solution.py:28
  92.3 5.3 %copy-start.15 = (s32[256]{0:T(256)S(1)}, s32[256]{0:T(256)}, u32[]{:S(2)}) copy-start(s32[256]{0:T(256)} %copy-done.14) | copy-start | bytes 3076
  92.3 5.0 %collective-permute-start.5 = (bf16[128,512]{1,0:T(8,128)(2,1)S(1)}, bf16[128,512]{1,0:T(8,128)(2,1)S(1)}, u32[]{:S(2)}, u32[]{:S(2)}) collective-permute-start(bf16[128,512]{1,0:T(8,128)(2,1)S(1)} %get-tuple-element.19), channel_id=1, source_target_pairs={{4,0},{8,4},{12,8},{16,12},{20,16},{24,20},{28,24},{0,28},{5,1},{9... | collective-permute-start | bytes 393224 | tf_op jit(solution)/shard_map/ppermute | solution.py:29
Sparse Core Ops, SparseCore 0:
  59.1 17.8 reduce-scatter.1
